TPU v7x, 32 devices: a whole 2x2x4 slice. The times are simulated.
32 devices in a mesh: dp: 8 (over y, x, core), tensor: 4 (over z).
Axes of the slice: x: 2, y: 2, z: 4, core: 2. Of those that a mesh axis runs over, the one named last changes fastest.
Arguments:
- tokens: bfloat16 [8192, 2048], P(('dp', 'tensor')), may hold values from -6 to 6
- positions: int32 [8192], P('dp'), may hold values from 0 to 1023, as said below
- norm_gain: float32 [2, 2, 2048], replicated, may hold values from 0.25 to 1.75
- norm_bias: float32 [2, 2, 2048], replicated, may hold values from -3 to 3
- w_qkv: bfloat16 [2, 2048, 3, 2048], P(None, 'dp', None, 'tensor'), may hold values from -0.125 to 0.125
- b_qkv: float32 [2, 3, 2048], replicated, may hold values from -3 to 3
- w_out: bfloat16 [2, 2048, 2048], P(None, 'tensor', 'dp'), may hold values from -0.5 to 0.5
- w_gate_up: bfloat16 [2, 2048, 2, 5632], P(None, 'dp', None, 'tensor'), may hold values from -0.125 to 0.125
- w_down: bfloat16 [2, 5632, 2048], P(None, 'tensor', 'dp'), may hold values from -0.078125 to 0.078125
- cotangent: bfloat16 [8192, 2048], P(('dp', 'tensor')), may hold values from -6 to 6
Outputs:
- activations: bfloat16 [8192, 2048], P(('dp', 'tensor'))
- input_grad: float32 [8192, 2048], P(('dp', 'tensor'))
- gain_grad: float32 [2, 2, 2048], replicated
- norm_bias_grad: float32 [2, 2, 2048], replicated
- qkv_grad: float32 [2, 2048, 3, 2048], P(None, 'dp', None, 'tensor')
- qkv_bias_grad: float32 [2, 3, 2048], replicated
- out_grad: float32 [2, 2048, 2048], P(None, 'tensor', 'dp')
- gate_up_grad: float32 [2, 2048, 2, 5632], P(None, 'dp', None, 'tensor')
- down_grad: float32 [2, 5632, 2048], P(None, 'tensor', 'dp')
Inputs may be any that keep to these rules, and one draw needn't show every extreme that they name: positions[i] counts the tokens before i in its document; documents lie end to end in the sequences of 1024 tokens, so the first token of a sequence has 0 and every other token has 0 or one more than the token before it.
All inputs are finite; a program needn't handle non-finite values.
Results may differ from a plain program's by a relative error of at most 0.023.
Values may be sent and summed in bfloat16 or wider, within the bound.
A program may use at most 320 MiB of HBM per device.

v0:
```python
import math
import jax
import jax.numpy as jnp
from jax import lax
from jax.sharding import PartitionSpec as P

HD = 64
ROT = 16
LAYERS = 2
norm_eps = 1e-05
theta_log = math.log(10000.0)
masked_score = -1e30
contract_rows = (((0,), (0,)), ((), ()))
contract_cols = (((1,), (1,)), ((), ()))


def norm_parts(hidden):
    average = jnp.mean(hidden, axis=-1, keepdims=True)
    centred = hidden - average
    variance = jnp.mean(centred * centred, axis=-1, keepdims=True)
    inverse = lax.rsqrt(variance + norm_eps)
    return (centred * inverse, inverse)


def norm_back(grad_normed, scaled, inverse, norm_weight):
    weighted = grad_normed * norm_weight
    first_mean = jnp.mean(weighted, axis=-1, keepdims=True)
    second_mean = jnp.mean(weighted * scaled, axis=-1, keepdims=True)
    grad_input = inverse * (weighted - first_mean - scaled * second_mean)
    return (grad_input, jnp.sum(grad_normed * scaled, axis=0), jnp.sum(grad_normed, axis=0))


def rotary_tables(positions):
    half_rot = ROT // 2
    frequency = jnp.exp(-(jnp.arange(half_rot, dtype=jnp.float32) * 2.0 / ROT) * theta_log)
    angles = positions.astype(jnp.float32)[:, None] * frequency[None, :]
    return (jnp.cos(angles)[:, None, :], jnp.sin(angles)[:, None, :])


def rotate(values, cos_table, sin_table):
    half_rot = ROT // 2
    first_half = values[..., :half_rot]
    second_half = values[..., half_rot:ROT]
    return jnp.concatenate(
        [
            first_half * cos_table - second_half * sin_table,
            second_half * cos_table + first_half * sin_table,
            values[..., ROT:],
        ],
        axis=-1,
    )


def inner_rows(left, right):
    return lax.dot_general(left, right, contract_rows, preferred_element_type=jnp.float32)


def inner_cols(left, right):
    return lax.dot_general(left, right, contract_cols, preferred_element_type=jnp.float32)


def block_scores(queries, key_rows, positions, number, block_rows, score_scale):
    seq_len = key_rows.shape[0]
    row_start = number * block_rows
    query_block = lax.dynamic_slice_in_dim(queries, row_start, block_rows, 0)
    scores = (
        jnp.einsum("qhd,khd->hqk", query_block, key_rows, preferred_element_type=jnp.float32)
        * score_scale
    )
    row_index = row_start + jnp.arange(block_rows, dtype=jnp.int32)
    first_key = row_index - lax.dynamic_slice_in_dim(positions, row_start, block_rows, 0)
    columns = jnp.arange(seq_len, dtype=jnp.int32)
    allowed = (columns[None, :] <= row_index[:, None]) & (columns[None, :] >= first_key[:, None])
    return (query_block, allowed, jnp.where(allowed[None], scores, masked_score))


def attend_forward(queries, key_rows, values, positions, score_scale):
    seq_len = queries.shape[0]
    block_rows = min(512, seq_len)

    def one_block(number):
        query_block, allowed, scores = block_scores(
            queries, key_rows, positions, number, block_rows, score_scale
        )
        row_max = jnp.max(scores, axis=-1, keepdims=True)
        shifted = jnp.exp(scores - row_max)
        row_sum = jnp.sum(shifted, axis=-1, keepdims=True)
        weights_low = (shifted / row_sum).astype(jnp.bfloat16)
        block_out = jnp.einsum(
            "hqk,khd->qhd", weights_low, values, preferred_element_type=jnp.float32
        )
        return (block_out, row_max + jnp.log(row_sum))

    block_outs, logsums = lax.map(one_block, jnp.arange(seq_len // block_rows, dtype=jnp.int32))
    return (block_outs.reshape(seq_len, -1), logsums)


def attend_back(queries, key_rows, values, positions, logsums, grad_attended, score_scale):
    seq_len = queries.shape[0]
    block_rows = min(512, seq_len)

    def one_block(totals, inputs):
        grad_keys, grad_values = totals
        number, logsum = inputs
        query_block, allowed, scores = block_scores(
            queries, key_rows, positions, number, block_rows, score_scale
        )
        softmax_rows = jnp.exp(scores - logsum)
        grad_block = lax.dynamic_slice_in_dim(grad_attended, number * block_rows, block_rows, 0)
        grad_probs = jnp.einsum(
            "qhd,khd->hqk", grad_block, values, preferred_element_type=jnp.float32
        )
        grad_values = grad_values + jnp.einsum(
            "hqk,qhd->khd",
            softmax_rows.astype(jnp.bfloat16),
            grad_block,
            preferred_element_type=jnp.float32,
        )
        row_inner = jnp.sum(softmax_rows * grad_probs, axis=-1, keepdims=True)
        grad_scores = jnp.where(allowed[None], softmax_rows * (grad_probs - row_inner), 0.0).astype(
            jnp.bfloat16
        )
        grad_query = (
            jnp.einsum("hqk,khd->qhd", grad_scores, key_rows, preferred_element_type=jnp.float32)
            * score_scale
        )
        grad_keys = (
            grad_keys
            + jnp.einsum(
                "hqk,qhd->khd", grad_scores, query_block, preferred_element_type=jnp.float32
            )
            * score_scale
        )
        return ((grad_keys, grad_values), grad_query)

    empty_grad = jnp.zeros(key_rows.shape, jnp.float32)
    numbers = jnp.arange(seq_len // block_rows, dtype=jnp.int32)
    (grad_keys, grad_values), grad_queries = lax.scan(
        one_block, (empty_grad, empty_grad), (numbers, logsums)
    )
    return (grad_queries.reshape(queries.shape), grad_keys, grad_values)


def per_device(
    tokens, positions, norm_gain, norm_bias, w_qkv, b_qkv, w_out, w_gate_up, w_down, cotangent
):
    tensor_rank = lax.axis_index("tensor")
    width_local = w_qkv.shape[3]
    heads_local = width_local // HD
    ff_local = w_gate_up.shape[3]
    local_rows = tokens.shape[0]
    seq_len = positions.shape[0]
    score_scale = 1.0 / math.sqrt(HD)
    cos_table, sin_table = rotary_tables(positions)
    hidden = tokens.astype(jnp.float32)
    kept_state = []
    for layer_index in range(LAYERS):
        gathered = (
            lax.all_gather(w_qkv[layer_index], "dp", axis=0, tiled=True),
            lax.all_gather(w_out[layer_index], "dp", axis=1, tiled=True),
            lax.all_gather(w_gate_up[layer_index], "dp", axis=0, tiled=True),
            lax.all_gather(w_down[layer_index], "dp", axis=1, tiled=True),
        )
        full_qkv, full_out, full_gu, full_down = gathered
        scaled_a, inverse_a = norm_parts(hidden)
        normed_a = (scaled_a * norm_gain[layer_index, 0] + norm_bias[layer_index, 0]).astype(
            jnp.bfloat16
        )
        rows_a = lax.all_gather(normed_a, "tensor", axis=0, tiled=True)
        bias_local = lax.dynamic_slice_in_dim(
            b_qkv[layer_index], tensor_rank * width_local, width_local, 1
        )
        mixed = jnp.dot(
            rows_a,
            full_qkv.reshape(full_qkv.shape[0], 3 * width_local),
            preferred_element_type=jnp.float32,
        ) + bias_local.reshape(3 * width_local)
        mixed = mixed.reshape(seq_len, 3, heads_local, HD)
        queries = rotate(mixed[:, 0], cos_table, sin_table).astype(jnp.bfloat16)
        key_rows = rotate(mixed[:, 1], cos_table, sin_table).astype(jnp.bfloat16)
        values = mixed[:, 2].astype(jnp.bfloat16)
        attended, logsums = attend_forward(queries, key_rows, values, positions, score_scale)
        attended = attended.astype(jnp.bfloat16)

        def project_attn(row_start, row_count, source=attended, weight=full_out):
            return jnp.dot(source, weight, preferred_element_type=jnp.float32)

        branch_a = lax.psum_scatter(
            project_attn(jnp.int32(0), local_rows * lax.axis_size("tensor")).astype(jnp.bfloat16),
            "tensor",
            scatter_dimension=0,
            tiled=True,
        ).astype(jnp.float32)
        hidden_mid = hidden + branch_a
        scaled_b, inverse_b = norm_parts(hidden_mid)
        normed_b = (scaled_b * norm_gain[layer_index, 1] + norm_bias[layer_index, 1]).astype(
            jnp.bfloat16
        )
        rows_b = lax.all_gather(normed_b, "tensor", axis=0, tiled=True)
        gate_up = jnp.dot(
            rows_b,
            full_gu.reshape(full_gu.shape[0], 2 * ff_local),
            preferred_element_type=jnp.float32,
        ).reshape(seq_len, 2, ff_local)
        activated = (jax.nn.silu(gate_up[:, 0]) * gate_up[:, 1]).astype(jnp.bfloat16)

        def project_mlp(row_start, row_count, source=activated, weight=full_down):
            return jnp.dot(source, weight, preferred_element_type=jnp.float32)

        hidden = hidden_mid + lax.psum_scatter(
            project_mlp(jnp.int32(0), local_rows * lax.axis_size("tensor")).astype(jnp.bfloat16),
            "tensor",
            scatter_dimension=0,
            tiled=True,
        ).astype(jnp.float32)
        kept_state.append(
            (
                gathered,
                scaled_a,
                inverse_a,
                rows_a,
                queries,
                key_rows,
                values,
                logsums,
                attended,
                scaled_b,
                inverse_b,
                rows_b,
                gate_up,
                activated,
            )
        )
    activations = hidden.astype(jnp.bfloat16)
    grad = cotangent.astype(jnp.float32)
    weight_parts = [None] * LAYERS
    gain_rows = [None] * LAYERS
    shift_rows = [None] * LAYERS
    qkv_shift_rows = [None] * LAYERS
    for layer_index in reversed(range(LAYERS)):
        (
            gathered,
            scaled_a,
            inverse_a,
            rows_a,
            queries,
            key_rows,
            values,
            logsums,
            attended,
            scaled_b,
            inverse_b,
            rows_b,
            gate_up,
            activated,
        ) = kept_state[layer_index]
        full_qkv, full_out, full_gu, full_down = (
            lax.all_gather(w_qkv[layer_index], "dp", axis=0, tiled=True),
            lax.all_gather(w_out[layer_index], "dp", axis=1, tiled=True),
            lax.all_gather(w_gate_up[layer_index], "dp", axis=0, tiled=True),
            lax.all_gather(w_down[layer_index], "dp", axis=1, tiled=True),
        )
        grad_rows_b = lax.all_gather(grad.astype(jnp.bfloat16), "tensor", axis=0, tiled=True)
        grad_down_weight = inner_rows(activated, grad_rows_b)
        grad_act = inner_cols(grad_rows_b, full_down)
        gate_part = gate_up[:, 0]
        up_part = gate_up[:, 1]
        sigmoid_gate = jax.nn.sigmoid(gate_part)
        grad_gate = grad_act * up_part * sigmoid_gate * (1.0 + gate_part * (1.0 - sigmoid_gate))
        grad_up = grad_act * jax.nn.silu(gate_part)
        grad_gate_up = (
            jnp.stack([grad_gate, grad_up], axis=1)
            .astype(jnp.bfloat16)
            .reshape(seq_len, 2 * ff_local)
        )
        grad_gu_weight = inner_rows(rows_b, grad_gate_up).reshape(full_gu.shape)
        flat_gu = full_gu.reshape(full_gu.shape[0], 2 * ff_local)

        def back_mlp(row_start, row_count, source=grad_gate_up, weight=flat_gu):
            return inner_cols(source, weight)

        grad_normed_b = lax.psum_scatter(
            back_mlp(jnp.int32(0), local_rows * lax.axis_size("tensor")).astype(jnp.bfloat16),
            "tensor",
            scatter_dimension=0,
            tiled=True,
        ).astype(jnp.float32)
        grad_in_b, gain_b, shift_b = norm_back(
            grad_normed_b, scaled_b, inverse_b, norm_gain[layer_index, 1]
        )
        grad = grad + grad_in_b
        grad_rows_a = lax.all_gather(grad.astype(jnp.bfloat16), "tensor", axis=0, tiled=True)
        grad_out_weight = inner_rows(attended, grad_rows_a)
        grad_attended = inner_cols(grad_rows_a, full_out).astype(jnp.bfloat16)
        grad_attended = grad_attended.reshape(seq_len, heads_local, HD)
        grad_queries, grad_keys, grad_values = attend_back(
            queries, key_rows, values, positions, logsums, grad_attended, score_scale
        )
        grad_queries = rotate(grad_queries, cos_table, -sin_table)
        grad_keys = rotate(grad_keys, cos_table, -sin_table)
        grad_mixed = jnp.stack([grad_queries, grad_keys, grad_values], axis=1)
        grad_mixed = grad_mixed.reshape(seq_len, 3 * width_local).astype(jnp.bfloat16)
        qkv_shift_local = jnp.sum(grad_mixed, axis=0, dtype=jnp.float32).reshape(3, width_local)
        qkv_shift_rows[layer_index] = lax.dynamic_update_slice(
            jnp.zeros((3, b_qkv.shape[2]), jnp.float32),
            qkv_shift_local,
            (jnp.int32(0), tensor_rank * width_local),
        )
        grad_qkv_weight = inner_rows(rows_a, grad_mixed).reshape(full_qkv.shape)
        flat_qkv = full_qkv.reshape(full_qkv.shape[0], 3 * width_local)

        def back_attn(row_start, row_count, source=grad_mixed, weight=flat_qkv):
            return inner_cols(source, weight)

        grad_normed_a = lax.psum_scatter(
            back_attn(jnp.int32(0), local_rows * lax.axis_size("tensor")).astype(jnp.bfloat16),
            "tensor",
            scatter_dimension=0,
            tiled=True,
        ).astype(jnp.float32)
        grad_in_a, gain_a, shift_a = norm_back(
            grad_normed_a, scaled_a, inverse_a, norm_gain[layer_index, 0]
        )
        grad = grad + grad_in_a
        gain_rows[layer_index] = jnp.stack([gain_a, gain_b])
        shift_rows[layer_index] = jnp.stack([shift_a, shift_b])
        weight_parts[layer_index] = (
            lax.psum_scatter(
                grad_qkv_weight.astype(jnp.bfloat16), "dp", scatter_dimension=0, tiled=True
            ).astype(jnp.float32),
            lax.psum_scatter(
                grad_out_weight.astype(jnp.bfloat16), "dp", scatter_dimension=1, tiled=True
            ).astype(jnp.float32),
            lax.psum_scatter(
                grad_gu_weight.astype(jnp.bfloat16), "dp", scatter_dimension=0, tiled=True
            ).astype(jnp.float32),
            lax.psum_scatter(
                grad_down_weight.astype(jnp.bfloat16), "dp", scatter_dimension=1, tiled=True
            ).astype(jnp.float32),
        )
    stack_qkv = jnp.stack([weight_parts[number][0] for number in range(LAYERS)])
    stack_out = jnp.stack([weight_parts[number][1] for number in range(LAYERS)])
    stack_gu = jnp.stack([weight_parts[number][2] for number in range(LAYERS)])
    stack_down = jnp.stack([weight_parts[number][3] for number in range(LAYERS)])
    gain_grad, norm_bias_grad, qkv_bias_grad = lax.psum(
        (jnp.stack(gain_rows), jnp.stack(shift_rows), jnp.stack(qkv_shift_rows)), ("dp", "tensor")
    )
    return (
        activations,
        grad,
        gain_grad,
        norm_bias_grad,
        stack_qkv,
        qkv_bias_grad,
        stack_out,
        stack_gu,
        stack_down,
    )


def solution(mesh):
    in_specs = (
        P(("dp", "tensor"), None),
        P("dp"),
        P(),
        P(),
        P(None, "dp", None, "tensor"),
        P(),
        P(None, "tensor", "dp"),
        P(None, "dp", None, "tensor"),
        P(None, "tensor", "dp"),
        P(("dp", "tensor"), None),
    )
    out_specs = (
        P(("dp", "tensor"), None),
        P(("dp", "tensor"), None),
        P(),
        P(),
        P(None, "dp", None, "tensor"),
        P(),
        P(None, "tensor", "dp"),
        P(None, "dp", None, "tensor"),
        P(None, "tensor", "dp"),
    )
    return jax.shard_map(
        per_device, mesh=mesh, in_specs=in_specs, out_specs=out_specs, check_vma=False
    )
```

profile of v0, /device:TPU:1, one launch (start us, length us, event | category | flops | bytes accessed | tf_op | source)
XLA Modules:
  0.0 2722.3 jit_solution(6625782385930977792)
XLA Ops:
  20.9 78.1 %all-gather.25.cloned.1.call-done = bf16[1024,2048]{1,0:T(8,128)(2,1)} async-done(((bf16[256,2048]{1,0:T(8,128)(2,1)}), bf16[1024,2048]{1,0:T(8,128)(2,1)}) %all-gather.25.cloned.1.call-update) | async-done | bytes 4194320 | tf_op jit(solution)/shard_map/all_gather | solution.py:169
  99.0 48.1 %all-gather.41.cloned.1.call-done = bf16[1,2048,3,512]{1,3,2,0:T(8,128)(2,1)} async-done(((bf16[1,256,3,512]{1,3,2,0:T(8,128)(2,1)}), bf16[1,2048,3,512]{1,3,2,0:T(8,128)(2,1)}) %all-gather.41.cloned.1.call-update) | async-done | bytes 6291472 | tf_op jit(solution)/shard_map/all_gather | solution.py:159
  147.1 11.8 convolution_add_fusion.1
  171.9 31.3 %while.54 = (s32[]{:T(128)}, bf16[2,512,8,64]{1,3,2,0:T(8,128)(2,1)}, f32[2,8,512,1]{2,1,3,0:T(8,128)S(1)}, s32[2]{0:T(128)S(1)}, s32[1024]{0:T(1024)S(1)}, /*in...) while((s32[]{:T(128)}, ...), condition=%wide.region_5.6_spmd, body=%wide.region_2.5_spmd.sunk | while | flops 1125643264 | bytes 64628996 | solution.py:94
  219.9 70.5 %reduce-scatter.17.cloned.1.call-done = bf16[256,2048]{1,0:T(8,128)(2,1)} async-done(((bf16[1024,2048]{1,0:T(8,128)(2,1)}), bf16[256,2048]{1,0:T(8,128)(2,1)}) %reduce-scatter.17.cloned.1.call-update) | async-done | bytes 1048592 | tf_op jit(solution)/shard_map/reduce_scatter | solution.py:188
  298.2 63.4 %all-gather.45.cloned.1.call-done = bf16[1,2048,2,1408]{3,1,2,0:T(8,128)(2,1)} async-done(((bf16[1,256,2,1408]{3,1,2,0:T(8,128)(2,1)}), bf16[1,2048,2,1408]{3,1,2,0:T(8,128)(2,1)}) %all-gather.45.cloned.1.call-update) | async-done | bytes 11534352 | tf_op jit(solution)/shard_map/all_gather | solution.py:161
  361.6 15.7 copy.37
  377.3 66.7 %all-gather.27.cloned.1.call-done = bf16[1024,2048]{1,0:T(8,128)(2,1)} async-done(((bf16[256,2048]{1,0:T(8,128)(2,1)}), bf16[1024,2048]{1,0:T(8,128)(2,1)}) %all-gather.27.cloned.1.call-update) | async-done | bytes 4194320 | tf_op jit(solution)/shard_map/all_gather | solution.py:199
  444.0 17.3 fusion.96
  468.2 21.7 all-gather.47.cloned.1.call-done
  490.0 10.8 fusion.124
  503.3 74.1 %reduce-scatter.19.cloned.1.call-done = bf16[256,2048]{1,0:T(8,128)(2,1)} async-done(((bf16[1024,2048]{1,0:T(8,128)(2,1)}), bf16[256,2048]{1,0:T(8,128)(2,1)}) %reduce-scatter.19.cloned.1.call-update) | async-done | bytes 1048592 | tf_op jit(solution)/shard_map/reduce_scatter | solution.py:210
  583.4 43.5 %all-gather.49.cloned.1.call-done = bf16[1,2048,3,512]{1,3,2,0:T(8,128)(2,1)} async-done(((bf16[1,256,3,512]{1,3,2,0:T(8,128)(2,1)}), bf16[1,2048,3,512]{1,3,2,0:T(8,128)(2,1)}) %all-gather.49.cloned.1.call-update) | async-done | bytes 6291472 | tf_op jit(solution)/shard_map/all_gather | solution.py:159
  626.9 82.4 %all-gather.29.cloned.1.call-done = bf16[1024,2048]{1,0:T(8,128)(2,1)} async-done(((bf16[256,2048]{1,0:T(8,128)(2,1)}), bf16[1024,2048]{1,0:T(8,128)(2,1)}) %all-gather.29.cloned.1.call-update) | async-done | bytes 4194320 | tf_op jit(solution)/shard_map/all_gather | solution.py:169
  709.2 12.0 convolution_add_fusion
  735.0 33.6 %while.55 = (s32[]{:T(128)}, bf16[2,512,8,64]{1,3,2,0:T(8,128)(2,1)S(1)}, f32[2,8,512,1]{2,1,3,0:T(8,128)S(1)}, s32[2]{0:T(128)S(1)}, s32[1024]{0:T(1024)S(1)}, ...) while((s32[]{:T(128)}, ...), condition=%wide.region_15.16_spmd, body=%wide.region_12.15_spmd.sunk | while | flops 1125643264 | bytes 56240328 | solution.py:94
  779.1 72.6 %reduce-scatter.21.cloned.1.call-done = bf16[256,2048]{1,0:T(8,128)(2,1)} async-done(((bf16[1024,2048]{1,0:T(8,128)(2,1)}), bf16[256,2048]{1,0:T(8,128)(2,1)}) %reduce-scatter.21.cloned.1.call-update) | async-done | bytes 1048592 | tf_op jit(solution)/shard_map/reduce_scatter | solution.py:188
  857.2 65.2 %all-gather.53.cloned.1.call-done = bf16[1,2048,2,1408]{3,1,2,0:T(8,128)(2,1)} async-done(((bf16[1,256,2,1408]{3,1,2,0:T(8,128)(2,1)}), bf16[1,2048,2,1408]{3,1,2,0:T(8,128)(2,1)}) %all-gather.53.cloned.1.call-update) | async-done | bytes 11534352 | tf_op jit(solution)/shard_map/all_gather | solution.py:161
  922.4 15.6 copy.42
  938.0 66.9 %all-gather.31.cloned.1.call-done = bf16[1024,2048]{1,0:T(8,128)(2,1)} async-done(((bf16[256,2048]{1,0:T(8,128)(2,1)}), bf16[1024,2048]{1,0:T(8,128)(2,1)}) %all-gather.31.cloned.1.call-update) | async-done | bytes 4194320 | tf_op jit(solution)/shard_map/all_gather | solution.py:199
  1004.8 18.8 fusion.94
  1023.7 62.0 %all-gather.33.cloned.1.call-done = bf16[1024,2048]{1,0:T(8,128)(2,1)} async-done(((bf16[256,2048]{1,0:T(8,128)(2,1)}), bf16[1024,2048]{1,0:T(8,128)(2,1)}) %all-gather.33.cloned.1.call-update) | async-done | bytes 4194320 | tf_op jit(solution)/shard_map/all_gather | solution.py:263
  1085.7 45.2 %all-gather.55.cloned.1.call-done = bf16[1,1408,2048]{2,1,0:T(8,128)(2,1)} async-done(((bf16[1,1408,256]{2,1,0:T(8,128)(2,1)}), bf16[1,1408,2048]{2,1,0:T(8,128)(2,1)}) %all-gather.55.cloned.1.call-update) | async-done | bytes 5767184 | tf_op jit(solution)/shard_map/all_gather | solution.py:162
  1130.9 14.1 multiply_bitcast_fusion.3
  1147.5 16.3 bitcast_convert_fusion.1
  1171.0 10.9 fusion.127
  1182.0 58.3 %reduce-scatter.25.cloned.1.call-done = bf16[256,2048]{1,0:T(8,128)(2,1)} async-done(((bf16[1024,2048]{1,0:T(8,128)(2,1)}), bf16[256,2048]{1,0:T(8,128)(2,1)}) %reduce-scatter.25.cloned.1.call-update) | async-done | bytes 1048592 | tf_op jit(solution)/shard_map/reduce_scatter | solution.py:282
  1243.1 76.6 %reduce-scatter.23.cloned.1.call-done = bf16[256,2048]{1,0:T(8,128)(2,1)} async-done(((bf16[1024,2048]{1,0:T(8,128)(2,1)}), bf16[256,2048]{1,0:T(8,128)(2,1)}) %reduce-scatter.23.cloned.1.call-update) | async-done | bytes 1048592 | tf_op jit(solution)/shard_map/reduce_scatter | solution.py:210
  1324.5 81.3 %all-gather.35.cloned.1.call-done = bf16[1024,2048]{1,0:T(8,128)(2,1)} async-done(((bf16[256,2048]{1,0:T(8,128)(2,1)}), bf16[1024,2048]{1,0:T(8,128)(2,1)}) %all-gather.35.cloned.1.call-update) | async-done | bytes 4194320 | tf_op jit(solution)/shard_map/all_gather | solution.py:292
  1414.1 183.7 %while.56 = (s32[]{:T(128)}, f32[1024,8,64]{0,2,1:T(8,128)}, f32[1024,8,64]{0,2,1:T(8,128)S(1)}, f32[2,512,8,64]{1,0,3,2:T(2,128)}, s32[2]{0:T(128)S(1)}, /*inde...) while((s32[]{:T(128)}, f32[1024,8,64]{0,2,1:T(8,128)}, ...), condition=%wide.region_25.26_spmd.clone, body=%wide.region_23.25_spmd.clone.sunk | while | flops 2747542528 | bytes 239134992 | solution.py:138
  1427.9 9.5 fusion.301
  1437.5 22.9 fusion.302
  1460.4 23.3 bitcast_add_fusion.8
  1486.1 19.6 dynamic_update_slice.48
  1519.3 9.6 fusion.301
  1528.8 22.9 fusion.302
  1551.8 23.9 bitcast_add_fusion.8
  1578.0 19.6 dynamic_update_slice.48
  1618.3 75.4 %reduce-scatter.27.cloned.1.call-done = bf16[256,2048]{1,0:T(8,128)(2,1)} async-done(((bf16[1024,2048]{1,0:T(8,128)(2,1)}), bf16[256,2048]{1,0:T(8,128)(2,1)}) %reduce-scatter.27.cloned.1.call-update) | async-done | bytes 1048592 | tf_op jit(solution)/shard_map/reduce_scatter | solution.py:315
  1699.3 81.4 %all-gather.37.cloned.1.call-done = bf16[1024,2048]{1,0:T(8,128)(2,1)} async-done(((bf16[256,2048]{1,0:T(8,128)(2,1)}), bf16[1024,2048]{1,0:T(8,128)(2,1)}) %all-gather.37.cloned.1.call-update) | async-done | bytes 4194320 | tf_op jit(solution)/shard_map/all_gather | solution.py:263
  1780.7 14.5 multiply_bitcast_fusion.1
  1797.7 16.2 bitcast_convert_fusion
  1814.0 75.4 %reduce-scatter.29.cloned.1.call-done = bf16[256,2048]{1,0:T(8,128)(2,1)} async-done(((bf16[1024,2048]{1,0:T(8,128)(2,1)}), bf16[256,2048]{1,0:T(8,128)(2,1)}) %reduce-scatter.29.cloned.1.call-update) | async-done | bytes 1048592 | tf_op jit(solution)/shard_map/reduce_scatter | solution.py:282
  1895.4 10.7 convolution_convert_fusion.2
  1908.0 10.7 convolution_convert_fusion.3
  1933.9 19.1 convolution_convert_fusion
  1968.5 19.2 convolution_convert_fusion.1
  2010.9 198.1 %while.57 = (s32[]{:T(128)}, f32[1024,8,64]{0,2,1:T(8,128)}, f32[1024,8,64]{0,2,1:T(8,128)}, f32[2,512,8,64]{1,0,3,2:T(2,128)}, s32[2]{0:T(128)S(1)}, /*index=5*...) while((s32[]{:T(128)}, f32[1024,8,64]{0,2,1:T(8,128)}, ...), condition=%wide.region_34.35_spmd.clone, body=%wide.region_32.34_spmd.clone.sunk | while | flops 2747542528 | bytes 239134992 | solution.py:138
  2034.5 27.4 %fusion.315 = f32[1,512,8,64]{1,3,2,0:T(8,128)} fusion(bf16[1024,8,64]{0,2,1:T(8,128)(2,1)S(1)} %get-tuple-element.900, f32[8,512,1024]{2,1,0:T(8,128)} %copy-done.1, f32[8,512,1024]{2,1,0:T(8,128)} %fusion.314, pred[512,1024]{1,0:T(8,128)(4,1)S(1)} %fusion.313), kind=kOutput, calls=%fused_computation.87.clone.1 | convolution fusion | flops 558109696 | bytes 36175872 | tf_op jit(solution)/shard_map/while/body/eval_jaxpr/hqk,khd->qhd/dot_general | solution.py:124
  2061.9 24.7 bitcast_add_fusion.10
  2088.9 19.5 dynamic_update_slice.49
  2125.1 9.9 fusion.314
  2135.0 26.6 fusion.315
  2161.6 25.4 bitcast_add_fusion.10
  2189.3 19.7 dynamic_update_slice.49
  2230.2 11.1 convolution_convert_fusion.4
  2243.3 11.1 convolution_convert_fusion.5
  2259.2 22.5 reduce-scatter.41.cloned.1.call-done
  2290.9 35.7 %reduce-scatter.39.cloned.1.call-done = bf16[512,256]{1,0:T(8,128)(2,1)} async-done(((bf16[512,2048]{1,0:T(8,128)(2,1)}), bf16[512,256]{1,0:T(8,128)(2,1)}) %reduce-scatter.39.cloned.1.call-update) | async-done | bytes 262160 | tf_op jit(solution)/shard_map/reduce_scatter | solution.py:331
  2326.6 44.5 %reduce-scatter.37.cloned.1.call-done = bf16[512,256]{1,0:T(8,128)(2,1)} async-done(((bf16[512,2048]{1,0:T(8,128)(2,1)}), bf16[512,256]{1,0:T(8,128)(2,1)}) %reduce-scatter.37.cloned.1.call-update) | async-done | bytes 262160 | tf_op jit(solution)/shard_map/reduce_scatter | solution.py:331
  2373.2 77.0 %reduce-scatter.31.cloned.1.call-done = bf16[256,2048]{1,0:T(8,128)(2,1)} async-done(((bf16[1024,2048]{1,0:T(8,128)(2,1)}), bf16[256,2048]{1,0:T(8,128)(2,1)}) %reduce-scatter.31.cloned.1.call-update) | async-done | bytes 1048592 | tf_op jit(solution)/shard_map/reduce_scatter | solution.py:315
  2457.2 58.6 %reduce-scatter.35.cloned.1.call-done = bf16[256,3,512]{2,0,1:T(8,128)(2,1)} async-done(((bf16[2048,3,512]{2,0,1:T(8,128)(2,1)}), bf16[256,3,512]{2,0,1:T(8,128)(2,1)}) %reduce-scatter.35.cloned.1.call-update) | async-done | bytes 786448 | tf_op jit(solution)/shard_map/reduce_scatter | solution.py:328
  2515.8 65.6 %reduce-scatter.33.cloned.1.call-done = bf16[256,3,512]{2,0,1:T(8,128)(2,1)} async-done(((bf16[2048,3,512]{2,0,1:T(8,128)(2,1)}), bf16[256,3,512]{2,0,1:T(8,128)(2,1)}) %reduce-scatter.33.cloned.1.call-update) | async-done | bytes 786448 | tf_op jit(solution)/shard_map/reduce_scatter | solution.py:328
  2584.6 126.3 %all-reduce.3.cloned.1.call-done = (f32[2,2,2048]{2,1,0:T(2,128)}, f32[2,2,2048]{2,1,0:T(2,128)}, f32[2,3,2048]{2,0,1:T(2,128)}) async-done(((f32[2,2,2048]{2,1,0:T(2,128)}, f32[2,2,2048]{2,1,0:T(2,128)}, f32[2,3,2048]{2,0,1:T(2,128)}), (f32[2,2,2048]{2,1,0:T(2,128)}, f32[2,2,2048]{2,1,0:T(2,128)}, f32[2,3,2048]{2,0,1:T(2,128)})) %all-reduce.3.cloned.1.call-update) | async-done | bytes 114704 | tf_op jit(solution)/shard_map/psum | solution.py:345
  (467 shorter events, 400.4 us)
Async XLA Ops:
  7.2 91.8 %all-gather.25.cloned.1.call-start = ((), (), s32[]{:S(2)}) async-start(), calls=%async_computation.16 | async-start | bytes 5242880 | tf_op jit(solution)/shard_map/all_gather | solution.py:169
  16.0 131.1 %all-gather.41.cloned.1.call-start = ((), (), s32[]{:S(2)}) async-start(), calls=%async_computation.40 | async-start | bytes 7077888 | tf_op jit(solution)/shard_map/all_gather | solution.py:159
  18.4 189.1 %all-gather.43.cloned.1.call-start = ((), (), s32[]{:S(2)}) async-start(), calls=%async_computation.41 | async-start | bytes 2359296 | tf_op jit(solution)/shard_map/all_gather | solution.py:160
  19.3 271.1 %reduce-scatter.17.cloned.1.call-start = ((), (), s32[]{:S(2)}) async-start(), calls=%async_computation.17 | async-start | bytes 5242880 | tf_op jit(solution)/shard_map/reduce_scatter | solution.py:188
  20.9 149.5 %copy-start.47 = (f32[1024,8]{0,1:T(8,128)}, f32[1024,8]{0,1:T(8,128)S(1)}, u32[]{:S(2)}) copy-start(f32[1024,8]{0,1:T(8,128)S(1)} %get-tuple-element.487) | copy-start | bytes 98308
  20.9 149.5 %copy-start.61 = (f32[1024,8]{0,1:T(8,128)}, f32[1024,8]{0,1:T(8,128)S(1)}, u32[]{:S(2)}) copy-start(f32[1024,8]{0,1:T(8,128)S(1)} %get-tuple-element.486) | copy-start | bytes 98308
  203.2 10.7 copy-start.5
  203.2 10.7 copy-start.12
  213.9 147.6 %all-gather.45.cloned.1.call-start = ((), (), s32[]{:S(2)}) async-start(), calls=%async_computation.42 | async-start | bytes 12976128 | tf_op jit(solution)/shard_map/all_gather | solution.py:161
  218.6 71.8 %copy-start.2 = (bf16[256,2048]{1,0:T(8,128)(2,1)S(1)}, bf16[256,2048]{1,0:T(8,128)(2,1)}, u32[]{:S(2)}) copy-start(bf16[256,2048]{1,0:T(8,128)(2,1)} %param.18) | copy-start | bytes 3145732
  219.9 74.7 %copy-start.65 = (f32[1,1,2048]{2,1,0:T(1,128)S(1)}, f32[1,1,2048]{2,1,0:T(1,128)}, u32[]{:S(2)}) copy-start(f32[1,1,2048]{2,1,0:T(1,128)} %get-tuple-element.478) | copy-start | bytes 24580
  219.9 224.1 %all-gather.27.cloned.1.call-start = ((), (), s32[]{:S(2)}) async-start(), calls=%async_computation.18 | async-start | bytes 5242880 | tf_op jit(solution)/shard_map/all_gather | solution.py:199
  296.8 193.1 %all-gather.47.cloned.1.call-start = ((), (), s32[]{:S(2)}) async-start(), calls=%async_computation.43 | async-start | bytes 6488064 | tf_op jit(solution)/shard_map/all_gather | solution.py:162
  298.1 279.3 %reduce-scatter.19.cloned.1.call-start = ((), (), s32[]{:S(2)}) async-start(), calls=%async_computation.19 | async-start | bytes 5242880 | tf_op jit(solution)/shard_map/reduce_scatter | solution.py:210
  500.8 126.0 %all-gather.49.cloned.1.call-start = ((), (), s32[]{:S(2)}) async-start(), calls=%async_computation.44 | async-start | bytes 7077888 | tf_op jit(solution)/shard_map/all_gather | solution.py:159
  503.2 77.2 %copy-start.67 = (f32[1,1,2048]{2,1,0:T(1,128)S(1)}, f32[1,1,2048]{2,1,0:T(1,128)}, u32[]{:S(2)}) copy-start(f32[1,1,2048]{2,1,0:T(1,128)} %get-tuple-element.480) | copy-start | bytes 24580
  503.2 77.2 %copy-start.79 = (f32[1,1,2048]{2,1,0:T(1,128)S(1)}, f32[1,1,2048]{2,1,0:T(1,128)}, u32[]{:S(2)}) copy-start(f32[1,1,2048]{2,1,0:T(1,128)} %get-tuple-element.484) | copy-start | bytes 24580
  503.2 206.0 %all-gather.29.cloned.1.call-start = ((), (), s32[]{:S(2)}) async-start(), calls=%async_computation.20 | async-start | bytes 5242880 | tf_op jit(solution)/shard_map/all_gather | solution.py:169
  579.5 141.8 %copy-start.88 = (f32[256]{0:T(256)}, f32[256]{0:T(256)S(1)}, u32[]{:S(2)}) copy-start(f32[256]{0:T(256)S(1)} %add_rsqrt_fusion.1) | copy-start | bytes 3076
  581.9 188.2 %all-gather.51.cloned.1.call-start = ((), (), s32[]{:S(2)}) async-start(), calls=%async_computation.45 | async-start | bytes 2359296 | tf_op jit(solution)/shard_map/all_gather | solution.py:160
  582.6 269.1 %reduce-scatter.21.cloned.1.call-start = ((), (), s32[]{:S(2)}) async-start(), calls=%async_computation.21 | async-start | bytes 5242880 | tf_op jit(solution)/shard_map/reduce_scatter | solution.py:188
  776.4 75.3 %copy-start.8 = (f32[256,2048]{1,0:T(8,128)S(1)}, f32[256,2048]{1,0:T(8,128)}, u32[]{:S(2)}) copy-start(f32[256,2048]{1,0:T(8,128)} %copy-done.7) | copy-start | bytes 6291460
  776.4 145.9 %all-gather.53.cloned.1.call-start = ((), (), s32[]{:S(2)}) async-start(), calls=%async_computation.46 | async-start | bytes 12976128 | tf_op jit(solution)/shard_map/all_gather | solution.py:161
  779.0 75.5 %copy-start.69 = (f32[1,1,2048]{2,1,0:T(1,128)S(1)}, f32[1,1,2048]{2,1,0:T(1,128)}, u32[]{:S(2)}) copy-start(f32[1,1,2048]{2,1,0:T(1,128)} %get-tuple-element.477) | copy-start | bytes 24580
  779.1 75.5 %copy-start.78 = (f32[1,1,2048]{2,1,0:T(1,128)S(1)}, f32[1,1,2048]{2,1,0:T(1,128)}, u32[]{:S(2)}) copy-start(f32[1,1,2048]{2,1,0:T(1,128)} %get-tuple-element.481) | copy-start | bytes 24580
  779.1 225.8 %all-gather.31.cloned.1.call-start = ((), (), s32[]{:S(2)}) async-start(), calls=%async_computation.22 | async-start | bytes 5242880 | tf_op jit(solution)/shard_map/all_gather | solution.py:199
  856.0 229.7 %all-gather.33.cloned.1.call-start = ((), (), s32[]{:S(2)}) async-start(), calls=%async_computation.24 | async-start | bytes 5242880 | tf_op jit(solution)/shard_map/all_gather | solution.py:263
  856.6 274.3 %all-gather.55.cloned.1.call-start = ((), (), s32[]{:S(2)}) async-start(), calls=%async_computation.47 | async-start | bytes 6488064 | tf_op jit(solution)/shard_map/all_gather | solution.py:162
  857.1 383.2 %reduce-scatter.25.cloned.1.call-start = ((), (), s32[]{:S(2)}) async-start(), calls=%async_computation.25 | async-start | bytes 5242880 | tf_op jit(solution)/shard_map/reduce_scatter | solution.py:282
  1163.8 156.0 %reduce-scatter.23.cloned.1.call-start = ((), (), s32[]{:S(2)}) async-start(), calls=%async_computation.23 | async-start | bytes 5242880 | tf_op jit(solution)/shard_map/reduce_scatter | solution.py:210
  1181.9 58.4 %copy-start.11 = (f32[256,2048]{1,0:T(8,128)S(1)}, f32[256,2048]{1,0:T(8,128)}, u32[]{:S(2)}) copy-start(f32[256,2048]{1,0:T(8,128)} %copy-done.10) | copy-start | bytes 6291460
  1181.9 137.9 %copy-start.23 = (bf16[256,2048]{1,0:T(8,128)(2,1)S(1)}, bf16[256,2048]{1,0:T(8,128)(2,1)}, u32[]{:S(2)}) copy-start(bf16[256,2048]{1,0:T(8,128)(2,1)} %param.27) | copy-start | bytes 3145732
  1181.9 223.9 %all-gather.35.cloned.1.call-start = ((), (), s32[]{:S(2)}) async-start(), calls=%async_computation.26 | async-start | bytes 5242880 | tf_op jit(solution)/shard_map/all_gather | solution.py:292
  1324.5 369.3 %reduce-scatter.27.cloned.1.call-start = ((), (), s32[]{:S(2)}) async-start(), calls=%async_computation.27 | async-start | bytes 5242880 | tf_op jit(solution)/shard_map/reduce_scatter | solution.py:315
  1324.5 89.6 %copy-start.58 = (f32[2,8,512,1]{2,1,3,0:T(8,128)S(1)}, f32[2,8,512,1]{2,1,3,0:T(8,128)}, u32[]{:S(2)}) copy-start(f32[2,8,512,1]{2,1,3,0:T(8,128)} %copy-done.57) | copy-start | bytes 98308
  1618.2 75.5 %copy-start.9 = (f32[256,2048]{1,0:T(8,128)S(1)}, f32[256,2048]{1,0:T(8,128)}, u32[]{:S(2)}) copy-start(f32[256,2048]{1,0:T(8,128)} %copy-done.7) | copy-start | bytes 6291460
  1618.2 75.5 %copy-start.68 = (f32[1,1,2048]{2,1,0:T(1,128)S(1)}, f32[1,1,2048]{2,1,0:T(1,128)}, u32[]{:S(2)}) copy-start(f32[1,1,2048]{2,1,0:T(1,128)} %get-tuple-element.480) | copy-start | bytes 24580
  1618.2 75.5 %copy-start.83 = (f32[256]{0:T(256)S(1)}, f32[256]{0:T(256)}, u32[]{:S(2)}) copy-start(f32[256]{0:T(256)} %copy-done.82) | copy-start | bytes 3076
  1618.2 75.5 %copy-start.89 = (f32[256]{0:T(256)S(1)}, f32[256]{0:T(256)}, u32[]{:S(2)}) copy-start(f32[256]{0:T(256)} %copy-done.88) | copy-start | bytes 3076
  1618.3 162.4 %all-gather.37.cloned.1.call-start = ((), (), s32[]{:S(2)}) async-start(), calls=%async_computation.28 | async-start | bytes 5242880 | tf_op jit(solution)/shard_map/all_gather | solution.py:263
  1699.3 190.2 %reduce-scatter.29.cloned.1.call-start = ((), (), s32[]{:S(2)}) async-start(), calls=%async_computation.29 | async-start | bytes 5242880 | tf_op jit(solution)/shard_map/reduce_scatter | solution.py:282
  1813.9 75.5 %copy-start.3 = (bf16[256,2048]{1,0:T(8,128)(2,1)S(1)}, bf16[256,2048]{1,0:T(8,128)(2,1)}, u32[]{:S(2)}) copy-start(bf16[256,2048]{1,0:T(8,128)(2,1)} %param.18) | copy-start | bytes 3145732
  1813.9 75.5 %copy-start.15 = (bf16[256,2048]{1,0:T(8,128)(2,1)S(1)}, bf16[256,2048]{1,0:T(8,128)(2,1)}, u32[]{:S(2)}) copy-start(bf16[256,2048]{1,0:T(8,128)(2,1)} %reduce-scatter.17.cloned.1.call-done) | copy-start | bytes 3145732
  1813.9 75.5 %copy-start.66 = (f32[1,1,2048]{2,1,0:T(1,128)S(1)}, f32[1,1,2048]{2,1,0:T(1,128)}, u32[]{:S(2)}) copy-start(f32[1,1,2048]{2,1,0:T(1,128)} %get-tuple-element.478) | copy-start | bytes 24580
  1813.9 75.5 %copy-start.81 = (f32[256]{0:T(256)S(1)}, f32[256]{0:T(256)}, u32[]{:S(2)}) copy-start(f32[256]{0:T(256)} %copy-done.80) | copy-start | bytes 3076
  1813.9 75.5 %copy-start.87 = (f32[256]{0:T(256)S(1)}, f32[256]{0:T(256)}, u32[]{:S(2)}) copy-start(f32[256]{0:T(256)} %copy-done.86) | copy-start | bytes 3076
  1814.0 181.6 %all-gather.39.cloned.1.call-start = ((), (), s32[]{:S(2)}) async-start(), calls=%async_computation.30 | async-start | bytes 5242880 | tf_op jit(solution)/shard_map/all_gather | solution.py:292
  1895.4 359.9 %reduce-scatter.47.cloned.1.call-start = ((), (), s32[]{:S(2)}) async-start(), calls=%async_computation.39 | async-start | bytes 6488064 | tf_op jit(solution)/shard_map/reduce_scatter | solution.py:337
  1906.1 349.2 %reduce-scatter.45.cloned.1.call-start = ((), (), s32[]{:S(2)}) async-start(), calls=%async_computation.38 | async-start | bytes 6488064 | tf_op jit(solution)/shard_map/reduce_scatter | solution.py:337
  1918.7 340.5 %reduce-scatter.43.cloned.1.call-start = ((), (), s32[]{:S(2)}) async-start(), calls=%async_computation.37 | async-start | bytes 12976128 | tf_op jit(solution)/shard_map/reduce_scatter | solution.py:334
  1953.1 328.6 %reduce-scatter.41.cloned.1.call-start = ((), (), s32[]{:S(2)}) async-start(), calls=%async_computation.36 | async-start | bytes 12976128 | tf_op jit(solution)/shard_map/reduce_scatter | solution.py:334
  1987.7 338.8 %reduce-scatter.39.cloned.1.call-start = ((), (), s32[]{:S(2)}) async-start(), calls=%async_computation.35 | async-start | bytes 2359296 | tf_op jit(solution)/shard_map/reduce_scatter | solution.py:331
  1995.5 375.6 %reduce-scatter.37.cloned.1.call-start = ((), (), s32[]{:S(2)}) async-start(), calls=%async_computation.34 | async-start | bytes 2359296 | tf_op jit(solution)/shard_map/reduce_scatter | solution.py:331
  2001.5 448.7 %reduce-scatter.31.cloned.1.call-start = ((), (), s32[]{:S(2)}) async-start(), calls=%async_computation.31 | async-start | bytes 5242880 | tf_op jit(solution)/shard_map/reduce_scatter | solution.py:315
  2228.3 287.6 %reduce-scatter.35.cloned.1.call-start = ((), (), s32[]{:S(2)}) async-start(), calls=%async_computation.33 | async-start | bytes 7077888 | tf_op jit(solution)/shard_map/reduce_scatter | solution.py:328
  2241.3 340.1 %reduce-scatter.33.cloned.1.call-start = ((), (), s32[]{:S(2)}) async-start(), calls=%async_computation.32 | async-start | bytes 7077888 | tf_op jit(solution)/shard_map/reduce_scatter | solution.py:328
  2254.4 456.5 %all-reduce.3.cloned.1.call-start = ((), (), s32[]{:S(2)}) async-start(), calls=%async_computation.48 | async-start | bytes 229376 | tf_op jit(solution)/shard_map/psum | solution.py:345
  2283.9 166.3 %copy-start.4 = (bf16[256,2048]{1,0:T(8,128)(2,1)S(1)}, bf16[256,2048]{1,0:T(8,128)(2,1)}, u32[]{:S(2)}) copy-start(bf16[256,2048]{1,0:T(8,128)(2,1)} %param.18) | copy-start | bytes 3145732
  2283.9 166.3 %copy-start.64 = (f32[1,1,2048]{2,1,0:T(1,128)S(1)}, f32[1,1,2048]{2,1,0:T(1,128)}, u32[]{:S(2)}) copy-start(f32[1,1,2048]{2,1,0:T(1,128)} %copy-done.63) | copy-start | bytes 24580
  2283.9 166.3 %copy-start.85 = (f32[256]{0:T(256)S(1)}, f32[256]{0:T(256)}, u32[]{:S(2)}) copy-start(f32[256]{0:T(256)} %copy-done.84) | copy-start | bytes 3076
  2283.9 166.3 %copy-start.91 = (f32[256]{0:T(256)S(1)}, f32[256]{0:T(256)}, u32[]{:S(2)}) copy-start(f32[256]{0:T(256)} %copy-done.90) | copy-start | bytes 3076
  2290.9 161.6 %copy-start.75 = (f32[2048]{0:T(1024)S(1)}, f32[2048]{0:T(1024)}, u32[]{:S(2)}) copy-start(f32[2048]{0:T(1024)} %get-tuple-element.313) | copy-start | bytes 24580
  2290.9 161.6 %copy-start.74 = (f32[2048]{0:T(1024)S(1)}, f32[2048]{0:T(1024)}, u32[]{:S(2)}) copy-start(f32[2048]{0:T(1024)} %get-tuple-element.326) | copy-start | bytes 24580
  2290.9 163.0 %copy-start.21 = (f32[256,2048]{1,0:T(8,128)S(1)}, f32[256,2048]{1,0:T(8,128)}, u32[]{:S(2)}) copy-start(f32[256,2048]{1,0:T(8,128)} %get-tuple-element.413) | copy-start | bytes 6291460
  (69 other events, 269.0 us)
Sparse Core Ops, SparseCore 0:
  16.1 82.8 all-gather.24
  101.5 45.5 all-gather.40
  149.6 28.1 all-gather.42
  214.1 76.3 reduce-scatter.16
  292.9 68.5 all-gather.44
  363.6 80.3 all-gather.26
  446.6 43.2 all-gather.46
  501.0 76.3 reduce-scatter.18
  579.2 47.5 all-gather.48
  628.8 80.3 all-gather.28
  711.1 27.1 all-gather.50
  776.5 75.1 reduce-scatter.20
  853.8 68.5 all-gather.52
  924.5 80.3 all-gather.30
  1006.3 79.2 all-gather.32
  1087.5 43.2 all-gather.54
  1163.9 76.3 reduce-scatter.24
  1242.5 77.2 reduce-scatter.22
  1324.6 81.2 all-gather.34
  1618.4 75.2 reduce-scatter.26
  1699.4 81.2 all-gather.36
  1814.1 75.2 reduce-scatter.28
  1895.5 81.2 all-gather.38
  1980.4 57.5 reduce-scatter.46
  2041.5 59.0 reduce-scatter.44
  2104.3 86.8 reduce-scatter.42
  2194.9 86.7 reduce-scatter.40
  2285.3 41.1 reduce-scatter.38
  2329.9 41.1 reduce-scatter.36
  2373.3 76.8 reduce-scatter.30
  2453.6 62.1 reduce-scatter.34
  2519.6 61.7 reduce-scatter.32
  2587.8 123.0 all-reduce.2
where the time goes:
time: 2740 us; the launch traced here: 2720 us
  waiting for transfers between devices  1740 us (64%)
  matrix products  597 us (22%)
  local copies, waits for them, and re-layouts  255 us (9%)
  other arithmetic  105 us (4%)
    all_gather x4, waiting for transfers between devices, per_device(): lax.all_gather(grad.astype(jnp.bfloat16), 'tensor', axis=0, tiled=True)  225 us
    all_gather x2, waiting for transfers between devices, per_device(): rows_a = lax.all_gather(normed_a, 'tensor', axis=0, tiled=True)  160 us
    reduce_scatter x2, waiting for transfers between devices, per_device(): lax.psum_scatter(back_attn(jnp.int32(0), local_rows * lax.axis_size('tens...  152 us
    reduce_scatter x2, waiting for transfers between devices, per_device(): lax.psum_scatter(project_mlp(jnp.int32(0), local_rows * lax.axis_size('te...  151 us
    reduce_scatter x2, waiting for transfers between devices, per_device(): lax.psum_scatter(project_attn(jnp.int32(0), local_rows * lax.axis_size('t...  143 us
    reduce_scatter x2, waiting for transfers between devices, per_device(): lax.psum_scatter(back_mlp(jnp.int32(0), local_rows * lax.axis_size('tenso...  134 us
    all_gather x2, waiting for transfers between devices, per_device(): rows_b = lax.all_gather(normed_b, 'tensor', axis=0, tiled=True)  134 us
    all_gather x2, waiting for transfers between devices, per_device(): lax.all_gather(w_gate_up[layer_index], 'dp', axis=0, tiled=True)  129 us
  transfers between devices with their start and end apart: 33, of which 27 were waited for; matrix products, arithmetic and copies ran while one was open for 22% of the time, Pallas kernels for 0%

commit v1 on v0

--- a/solution.py
+++ b/solution.py
@@ -166,7 +166,26 @@
         normed_a = (scaled_a * norm_gain[layer_index, 0] + norm_bias[layer_index, 0]).astype(
             jnp.bfloat16
         )
-        rows_a = lax.all_gather(normed_a, "tensor", axis=0, tiled=True)
+        size, index, rows = (lax.axis_size("tensor"), lax.axis_index("tensor"), normed_a.shape[0])
+        upward = [(i, (i + 1) % size) for i in range(size)]
+        left_2 = [(i, (i - 1) % size) for i in range(size)]
+        out = jnp.zeros(
+            (*normed_a.shape[:0], size * rows, *normed_a.shape[0 + 1 :]), normed_a.dtype
+        )
+        out = lax.dynamic_update_slice_in_dim(out, normed_a, index * rows, axis=0)
+        from_left = from_right = normed_a
+        half = size // 2
+        for lap in range(1, half + 1):
+            from_left = lax.ppermute(from_left, "tensor", upward)
+            out = lax.dynamic_update_slice_in_dim(
+                out, from_left, (index - lap) % size * rows, axis=0
+            )
+            if lap < size - half:
+                from_right = lax.ppermute(from_right, "tensor", left_2)
+                out = lax.dynamic_update_slice_in_dim(
+                    out, from_right, (index + lap) % size * rows, axis=0
+                )
+        rows_a = out
         bias_local = lax.dynamic_slice_in_dim(
             b_qkv[layer_index], tensor_rank * width_local, width_local, 1
         )

time: 2740 us -> 2640 us (0.964)
  waiting for transfers between devices: 1740 us -> 1600 us
    all_gather x2 -> x0, waiting for transfers between devices: 160 us -> none  [per_device(): rows_a = lax.all_gather(normed_a, 'tensor', axis=0, tiled=True)]
    ppermute x0 -> x6, waiting for transfers between devices: none -> 112 us  [the longest x4 77.8 us: per_device(): from_left = lax.ppermute(from_left, 'tensor', upward)]
    all_gather x2, waiting for transfers between devices: 91.6 us -> 0.01 us  [per_device(): lax.all_gather(w_qkv[layer_index], 'dp', axis=0, tiled=True)]
  transfers between devices with their start and end apart: 33 -> 37, of which waited for: 27 -> 29; matrix products, arithmetic and copies ran while one was open for 22% -> 24% of each run, Pallas kernels for 0% -> 0%
where the time goes in v1:
time: 2640 us; the launch traced here: 2620 us
  waiting for transfers between devices  1600 us (61%)
  matrix products  597 us (23%)
  local copies, waits for them, and re-layouts  278 us (11%)
  other arithmetic  101 us (4%)
    all_gather x4, waiting for transfers between devices, per_device(): lax.all_gather(grad.astype(jnp.bfloat16), 'tensor', axis=0, tiled=True)  225 us
    reduce_scatter x2, waiting for transfers between devices, per_device(): lax.psum_scatter(back_attn(jnp.int32(0), local_rows * lax.axis_size('tens...  153 us
    reduce_scatter x2, waiting for transfers between devices, per_device(): lax.psum_scatter(project_mlp(jnp.int32(0), local_rows * lax.axis_size('te...  151 us
    reduce_scatter x2, waiting for transfers between devices, per_device(): lax.psum_scatter(project_attn(jnp.int32(0), local_rows * lax.axis_size('t...  147 us
    all_gather x2, waiting for transfers between devices, per_device(): rows_b = lax.all_gather(normed_b, 'tensor', axis=0, tiled=True)  134 us
    reduce_scatter x2, waiting for transfers between devices, per_device(): lax.psum_scatter(back_mlp(jnp.int32(0), local_rows * lax.axis_size('tenso...  134 us
    all_gather x2, waiting for transfers between devices, per_device(): lax.all_gather(w_gate_up[layer_index], 'dp', axis=0, tiled=True)  129 us
    psum x1, waiting for transfers between devices, per_device(): lax.psum((jnp.stack(gain_rows), jnp.stack(shift_rows), jnp.stack(qkv_shif...  126 us
  transfers between devices with their start and end apart: 37, of which 29 were waited for; matrix products, arithmetic and copies ran while one was open for 24% of the time, Pallas kernels for 0%

profile of v1, /device:TPU:1, one launch (start us, length us, event | category | flops | bytes accessed | tf_op | source)
XLA Modules:
  0.0 2624.1 jit_solution(6986607758530658549)
XLA Ops:
  21.0 19.6 collective-permute-done
  46.0 16.7 collective-permute-done.1
  66.4 17.7 collective-permute-done.2
  86.7 11.9 convolution_add_fusion.1
  111.2 42.5 %while.54 = (s32[]{:T(128)}, bf16[2,512,8,64]{1,3,2,0:T(8,128)(2,1)}, f32[2,8,512,1]{2,1,3,0:T(8,128)S(1)}, s32[2]{0:T(128)S(1)}, s32[1024]{0:T(1024)S(1)}, /*in...) while((s32[]{:T(128)}, ...), condition=%wide.region_5.6_spmd, body=%wide.region_2.5_spmd.sunk | while | flops 1125643264 | bytes 64628996 | solution.py:94
  170.5 72.4 %reduce-scatter.17.cloned.1.call-done = bf16[256,2048]{1,0:T(8,128)(2,1)} async-done(((bf16[1024,2048]{1,0:T(8,128)(2,1)}), bf16[256,2048]{1,0:T(8,128)(2,1)}) %reduce-scatter.17.cloned.1.call-update) | async-done | bytes 1048592 | tf_op jit(solution)/shard_map/reduce_scatter | solution.py:207
  250.4 63.6 %all-gather.39.cloned.1.call-done = bf16[1,2048,2,1408]{3,1,2,0:T(8,128)(2,1)} async-done(((bf16[1,256,2,1408]{3,1,2,0:T(8,128)(2,1)}), bf16[1,2048,2,1408]{3,1,2,0:T(8,128)(2,1)}) %all-gather.39.cloned.1.call-update) | async-done | bytes 11534352 | tf_op jit(solution)/shard_map/all_gather | solution.py:161
  314.0 15.4 copy.47
  329.4 67.1 %all-gather.23.cloned.1.call-done = bf16[1024,2048]{1,0:T(8,128)(2,1)} async-done(((bf16[256,2048]{1,0:T(8,128)(2,1)}), bf16[1024,2048]{1,0:T(8,128)(2,1)}) %all-gather.23.cloned.1.call-update) | async-done | bytes 4194320 | tf_op jit(solution)/shard_map/all_gather | solution.py:218
  396.5 17.3 fusion.96
  420.7 21.6 all-gather.41.cloned.1.call-done
  442.3 10.8 fusion.124
  455.5 74.2 %reduce-scatter.19.cloned.1.call-done = bf16[256,2048]{1,0:T(8,128)(2,1)} async-done(((bf16[1024,2048]{1,0:T(8,128)(2,1)}), bf16[256,2048]{1,0:T(8,128)(2,1)}) %reduce-scatter.19.cloned.1.call-update) | async-done | bytes 1048592 | tf_op jit(solution)/shard_map/reduce_scatter | solution.py:229
  536.5 22.6 collective-permute-done.3
  564.8 17.6 collective-permute-done.4
  586.2 17.9 collective-permute-done.5
  606.8 12.0 convolution_add_fusion
  632.4 34.0 %while.55 = (s32[]{:T(128)}, bf16[2,512,8,64]{1,3,2,0:T(8,128)(2,1)S(1)}, f32[2,8,512,1]{2,1,3,0:T(8,128)S(1)}, s32[2]{0:T(128)S(1)}, s32[1024]{0:T(1024)S(1)}, ...) while((s32[]{:T(128)}, ...), condition=%wide.region_15.16_spmd, body=%wide.region_12.15_spmd.sunk | while | flops 1125643264 | bytes 56240328 | solution.py:94
  676.9 74.2 %reduce-scatter.21.cloned.1.call-done = bf16[256,2048]{1,0:T(8,128)(2,1)} async-done(((bf16[1024,2048]{1,0:T(8,128)(2,1)}), bf16[256,2048]{1,0:T(8,128)(2,1)}) %reduce-scatter.21.cloned.1.call-update) | async-done | bytes 1048592 | tf_op jit(solution)/shard_map/reduce_scatter | solution.py:207
  756.8 65.0 %all-gather.47.cloned.1.call-done = bf16[1,2048,2,1408]{3,1,2,0:T(8,128)(2,1)} async-done(((bf16[1,256,2,1408]{3,1,2,0:T(8,128)(2,1)}), bf16[1,2048,2,1408]{3,1,2,0:T(8,128)(2,1)}) %all-gather.47.cloned.1.call-update) | async-done | bytes 11534352 | tf_op jit(solution)/shard_map/all_gather | solution.py:161
  821.8 15.6 copy.56
  837.4 66.9 %all-gather.25.cloned.1.call-done = bf16[1024,2048]{1,0:T(8,128)(2,1)} async-done(((bf16[256,2048]{1,0:T(8,128)(2,1)}), bf16[1024,2048]{1,0:T(8,128)(2,1)}) %all-gather.25.cloned.1.call-update) | async-done | bytes 4194320 | tf_op jit(solution)/shard_map/all_gather | solution.py:218
  904.3 18.8 fusion.94
  923.1 62.1 %all-gather.27.cloned.1.call-done = bf16[1024,2048]{1,0:T(8,128)(2,1)} async-done(((bf16[256,2048]{1,0:T(8,128)(2,1)}), bf16[1024,2048]{1,0:T(8,128)(2,1)}) %all-gather.27.cloned.1.call-update) | async-done | bytes 4194320 | tf_op jit(solution)/shard_map/all_gather | solution.py:282
  985.3 45.2 %all-gather.49.cloned.1.call-done = bf16[1,1408,2048]{2,1,0:T(8,128)(2,1)} async-done(((bf16[1,1408,256]{2,1,0:T(8,128)(2,1)}), bf16[1,1408,2048]{2,1,0:T(8,128)(2,1)}) %all-gather.49.cloned.1.call-update) | async-done | bytes 5767184 | tf_op jit(solution)/shard_map/all_gather | solution.py:162
  1030.5 14.1 multiply_bitcast_fusion.3
  1047.1 16.3 bitcast_convert_fusion.1
  1070.5 10.9 fusion.127
  1081.4 58.5 %reduce-scatter.25.cloned.1.call-done = bf16[256,2048]{1,0:T(8,128)(2,1)} async-done(((bf16[1024,2048]{1,0:T(8,128)(2,1)}), bf16[256,2048]{1,0:T(8,128)(2,1)}) %reduce-scatter.25.cloned.1.call-update) | async-done | bytes 1048592 | tf_op jit(solution)/shard_map/reduce_scatter | solution.py:301
  1142.8 76.6 %reduce-scatter.23.cloned.1.call-done = bf16[256,2048]{1,0:T(8,128)(2,1)} async-done(((bf16[1024,2048]{1,0:T(8,128)(2,1)}), bf16[256,2048]{1,0:T(8,128)(2,1)}) %reduce-scatter.23.cloned.1.call-update) | async-done | bytes 1048592 | tf_op jit(solution)/shard_map/reduce_scatter | solution.py:229
  1224.2 81.3 %all-gather.29.cloned.1.call-done = bf16[1024,2048]{1,0:T(8,128)(2,1)} async-done(((bf16[256,2048]{1,0:T(8,128)(2,1)}), bf16[1024,2048]{1,0:T(8,128)(2,1)}) %all-gather.29.cloned.1.call-update) | async-done | bytes 4194320 | tf_op jit(solution)/shard_map/all_gather | solution.py:311
  1313.7 183.9 %while.56 = (s32[]{:T(128)}, f32[1024,8,64]{0,2,1:T(8,128)}, f32[1024,8,64]{0,2,1:T(8,128)S(1)}, f32[2,512,8,64]{1,0,3,2:T(2,128)}, s32[2]{0:T(128)S(1)}, /*inde...) while((s32[]{:T(128)}, f32[1024,8,64]{0,2,1:T(8,128)}, ...), condition=%wide.region_25.26_spmd.clone, body=%wide.region_23.25_spmd.clone.sunk | while | flops 2747542528 | bytes 239134992 | solution.py:138
  1337.3 22.9 fusion.302
  1360.2 23.4 bitcast_add_fusion.8
  1385.9 19.6 dynamic_update_slice.88
  1428.7 22.9 fusion.302
  1451.6 23.9 bitcast_add_fusion.8
  1477.8 19.6 dynamic_update_slice.88
  1518.1 75.4 %reduce-scatter.27.cloned.1.call-done = bf16[256,2048]{1,0:T(8,128)(2,1)} async-done(((bf16[1024,2048]{1,0:T(8,128)(2,1)}), bf16[256,2048]{1,0:T(8,128)(2,1)}) %reduce-scatter.27.cloned.1.call-update) | async-done | bytes 1048592 | tf_op jit(solution)/shard_map/reduce_scatter | solution.py:334
  1600.3 81.4 %all-gather.31.cloned.1.call-done = bf16[1024,2048]{1,0:T(8,128)(2,1)} async-done(((bf16[256,2048]{1,0:T(8,128)(2,1)}), bf16[1024,2048]{1,0:T(8,128)(2,1)}) %all-gather.31.cloned.1.call-update) | async-done | bytes 4194320 | tf_op jit(solution)/shard_map/all_gather | solution.py:282
  1681.7 14.3 multiply_bitcast_fusion.1
  1698.4 16.2 bitcast_convert_fusion
  1714.7 75.4 %reduce-scatter.29.cloned.1.call-done = bf16[256,2048]{1,0:T(8,128)(2,1)} async-done(((bf16[1024,2048]{1,0:T(8,128)(2,1)}), bf16[256,2048]{1,0:T(8,128)(2,1)}) %reduce-scatter.29.cloned.1.call-update) | async-done | bytes 1048592 | tf_op jit(solution)/shard_map/reduce_scatter | solution.py:301
  1797.3 10.7 convolution_convert_fusion.2
  1810.0 10.7 convolution_convert_fusion.3
  1836.2 19.1 convolution_convert_fusion
  1870.5 19.2 convolution_convert_fusion.1
  1913.0 198.2 %while.57 = (s32[]{:T(128)}, f32[1024,8,64]{0,2,1:T(8,128)}, f32[1024,8,64]{0,2,1:T(8,128)}, f32[2,512,8,64]{1,0,3,2:T(2,128)}, s32[2]{0:T(128)S(1)}, /*index=5*...) while((s32[]{:T(128)}, f32[1024,8,64]{0,2,1:T(8,128)}, ...), condition=%wide.region_34.35_spmd.clone, body=%wide.region_32.34_spmd.clone.sunk | while | flops 2747542528 | bytes 239134992 | solution.py:138
  1936.7 27.5 %fusion.315 = f32[1,512,8,64]{1,3,2,0:T(8,128)} fusion(bf16[1024,8,64]{0,2,1:T(8,128)(2,1)S(1)} %get-tuple-element.900, f32[8,512,1024]{2,1,0:T(8,128)} %copy-done.1, f32[8,512,1024]{2,1,0:T(8,128)} %fusion.314, pred[512,1024]{1,0:T(8,128)(4,1)S(1)} %fusion.313), kind=kOutput, calls=%fused_computation.87.clone.1 | convolution fusion | flops 558109696 | bytes 36175872 | tf_op jit(solution)/shard_map/while/body/eval_jaxpr/hqk,khd->qhd/dot_general | solution.py:124
  1964.2 24.7 bitcast_add_fusion.10
  1991.2 19.6 dynamic_update_slice.89
  2027.3 9.9 fusion.314
  2037.2 26.6 %fusion.315 = f32[1,512,8,64]{1,3,2,0:T(8,128)} fusion(bf16[1024,8,64]{0,2,1:T(8,128)(2,1)S(1)} %get-tuple-element.900, f32[8,512,1024]{2,1,0:T(8,128)} %copy-done.1, f32[8,512,1024]{2,1,0:T(8,128)} %fusion.314, pred[512,1024]{1,0:T(8,128)(4,1)S(1)} %fusion.313), kind=kOutput, calls=%fused_computation.87.clone.1 | convolution fusion | flops 558109696 | bytes 36175872 | tf_op jit(solution)/shard_map/while/body/eval_jaxpr/hqk,khd->qhd/dot_general | solution.py:124
  2063.8 25.4 bitcast_add_fusion.10
  2091.5 19.7 dynamic_update_slice.89
  2132.8 10.9 convolution_convert_fusion.4
  2145.6 11.0 convolution_convert_fusion.5
  2161.5 22.4 reduce-scatter.41.cloned.1.call-done
  2193.1 35.5 %reduce-scatter.39.cloned.1.call-done = bf16[512,256]{1,0:T(8,128)(2,1)} async-done(((bf16[512,2048]{1,0:T(8,128)(2,1)}), bf16[512,256]{1,0:T(8,128)(2,1)}) %reduce-scatter.39.cloned.1.call-update) | async-done | bytes 262160 | tf_op jit(solution)/shard_map/reduce_scatter | solution.py:350
  2228.6 44.4 %reduce-scatter.37.cloned.1.call-done = bf16[512,256]{1,0:T(8,128)(2,1)} async-done(((bf16[512,2048]{1,0:T(8,128)(2,1)}), bf16[512,256]{1,0:T(8,128)(2,1)}) %reduce-scatter.37.cloned.1.call-update) | async-done | bytes 262160 | tf_op jit(solution)/shard_map/reduce_scatter | solution.py:350
  2275.0 77.1 %reduce-scatter.31.cloned.1.call-done = bf16[256,2048]{1,0:T(8,128)(2,1)} async-done(((bf16[1024,2048]{1,0:T(8,128)(2,1)}), bf16[256,2048]{1,0:T(8,128)(2,1)}) %reduce-scatter.31.cloned.1.call-update) | async-done | bytes 1048592 | tf_op jit(solution)/shard_map/reduce_scatter | solution.py:334
  2359.2 58.6 %reduce-scatter.35.cloned.1.call-done = bf16[256,3,512]{2,0,1:T(8,128)(2,1)} async-done(((bf16[2048,3,512]{2,0,1:T(8,128)(2,1)}), bf16[256,3,512]{2,0,1:T(8,128)(2,1)}) %reduce-scatter.35.cloned.1.call-update) | async-done | bytes 786448 | tf_op jit(solution)/shard_map/reduce_scatter | solution.py:347
  2417.8 65.4 %reduce-scatter.33.cloned.1.call-done = bf16[256,3,512]{2,0,1:T(8,128)(2,1)} async-done(((bf16[2048,3,512]{2,0,1:T(8,128)(2,1)}), bf16[256,3,512]{2,0,1:T(8,128)(2,1)}) %reduce-scatter.33.cloned.1.call-update) | async-done | bytes 786448 | tf_op jit(solution)/shard_map/reduce_scatter | solution.py:347
  2486.5 126.5 %all-reduce.3.cloned.1.call-done = (f32[2,2,2048]{2,1,0:T(2,128)}, f32[2,2,2048]{2,1,0:T(2,128)}, f32[2,3,2048]{2,0,1:T(2,128)}) async-done(((f32[2,2,2048]{2,1,0:T(2,128)}, f32[2,2,2048]{2,1,0:T(2,128)}, f32[2,3,2048]{2,0,1:T(2,128)}), (f32[2,2,2048]{2,1,0:T(2,128)}, f32[2,2,2048]{2,1,0:T(2,128)}, f32[2,3,2048]{2,0,1:T(2,128)})) %all-reduce.3.cloned.1.call-update) | async-done | bytes 114704 | tf_op jit(solution)/shard_map/psum | solution.py:364
  (487 shorter events, 446.0 us)
Async XLA Ops:
  7.2 79.5 %all-gather.35.cloned.1.call-start = ((), (), s32[]{:S(2)}) async-start(), calls=%async_computation.38 | async-start | bytes 7077888 | tf_op jit(solution)/shard_map/all_gather | solution.py:159
  10.9 147.1 %all-gather.37.cloned.1.call-start = ((), (), s32[]{:S(2)}) async-start(), calls=%async_computation.39 | async-start | bytes 2359296 | tf_op jit(solution)/shard_map/all_gather | solution.py:160
  13.4 27.1 %collective-permute-start = (bf16[256,2048]{1,0:T(8,128)(2,1)S(1)}, bf16[256,2048]{1,0:T(8,128)(2,1)S(1)}, u32[]{:S(2)}, u32[]{:S(2)}) collective-permute-start(bf16[256,2048]{1,0:T(8,128)(2,1)S(1)} %fusion.147), channel_id=1, source_target_pairs={{0,1},{1,2},{2,3},{3,0},{4,5},{5,6},{6,7},{7,4},{8,9},{9,10},{10,1... | collective-permute-start | bytes 3145736 | tf_op jit(solution)/shard_map/ppermute | solution.py:179
  15.6 47.0 %collective-permute-start.1 = (bf16[256,2048]{1,0:T(8,128)(2,1)S(1)}, bf16[256,2048]{1,0:T(8,128)(2,1)}, u32[]{:S(2)}, u32[]{:S(2)}) collective-permute-start(bf16[256,2048]{1,0:T(8,128)(2,1)S(1)} %fusion.147), channel_id=1, source_target_pairs={{0,3},{1,0},{2,1},{3,2},{4,7},{5,4},{6,5},{7,6},{8,11},{9,8},{10,9... | collective-permute-start | bytes 3145736 | tf_op jit(solution)/shard_map/ppermute | solution.py:184
  19.6 223.3 %reduce-scatter.17.cloned.1.call-start = ((), (), s32[]{:S(2)}) async-start(), calls=%async_computation.16 | async-start | bytes 5242880 | tf_op jit(solution)/shard_map/reduce_scatter | solution.py:207
  40.5 43.5 %collective-permute-start.2 = (bf16[256,2048]{1,0:T(8,128)(2,1)S(1)}, bf16[256,2048]{1,0:T(8,128)(2,1)}, u32[]{:S(2)}, u32[]{:S(2)}) collective-permute-start(bf16[256,2048]{1,0:T(8,128)(2,1)S(1)} %collective-permute-done), channel_id=1, source_target_pairs={{0,1},{1,2},{2,3},{3,0},{4,5},{5,6},{6,7},{7,4},{8,9},{9,10},{10,1... | collective-permute-start | bytes 3145736 | tf_op jit(solution)/shard_map/ppermute | solution.py:179
  41.4 68.4 %copy-start.57 = (f32[1024,8]{0,1:T(8,128)}, f32[1024,8]{0,1:T(8,128)S(1)}, u32[]{:S(2)}) copy-start(f32[1024,8]{0,1:T(8,128)S(1)} %get-tuple-element.486) | copy-start | bytes 98308
  164.4 78.5 %copy-start.3 = (bf16[256,2048]{1,0:T(8,128)(2,1)S(1)}, bf16[256,2048]{1,0:T(8,128)(2,1)}, u32[]{:S(2)}) copy-start(bf16[256,2048]{1,0:T(8,128)(2,1)} %param.18) | copy-start | bytes 3145732
  164.4 149.6 %all-gather.39.cloned.1.call-start = ((), (), s32[]{:S(2)}) async-start(), calls=%async_computation.40 | async-start | bytes 12976128 | tf_op jit(solution)/shard_map/all_gather | solution.py:161
  169.2 77.7 %copy-start.61 = (f32[1,1,2048]{2,1,0:T(1,128)S(1)}, f32[1,1,2048]{2,1,0:T(1,128)}, u32[]{:S(2)}) copy-start(f32[1,1,2048]{2,1,0:T(1,128)} %get-tuple-element.478) | copy-start | bytes 24580
  170.4 78.7 %copy-start.40 = (bf16[2,1408,256]{2,1,0:T(8,128)(2,1)S(1)}, bf16[2,1408,256]{2,1,0:T(8,128)(2,1)}, u32[]{:S(2)}) copy-start(bf16[2,1408,256]{2,1,0:T(8,128)(2,1)} %param.26) | copy-start | bytes 4325380
  170.5 226.0 %all-gather.23.cloned.1.call-start = ((), (), s32[]{:S(2)}) async-start(), calls=%async_computation.17 | async-start | bytes 5242880 | tf_op jit(solution)/shard_map/all_gather | solution.py:218
  249.1 193.1 %all-gather.41.cloned.1.call-start = ((), (), s32[]{:S(2)}) async-start(), calls=%async_computation.41 | async-start | bytes 6488064 | tf_op jit(solution)/shard_map/all_gather | solution.py:162
  250.4 279.3 %reduce-scatter.19.cloned.1.call-start = ((), (), s32[]{:S(2)}) async-start(), calls=%async_computation.18 | async-start | bytes 5242880 | tf_op jit(solution)/shard_map/reduce_scatter | solution.py:229
  453.1 153.6 %all-gather.43.cloned.1.call-start = ((), (), s32[]{:S(2)}) async-start(), calls=%async_computation.42 | async-start | bytes 7077888 | tf_op jit(solution)/shard_map/all_gather | solution.py:159
  455.4 77.3 %copy-start.63 = (f32[1,1,2048]{2,1,0:T(1,128)S(1)}, f32[1,1,2048]{2,1,0:T(1,128)}, u32[]{:S(2)}) copy-start(f32[1,1,2048]{2,1,0:T(1,128)} %get-tuple-element.480) | copy-start | bytes 24580
  455.4 77.3 %copy-start.75 = (f32[1,1,2048]{2,1,0:T(1,128)S(1)}, f32[1,1,2048]{2,1,0:T(1,128)}, u32[]{:S(2)}) copy-start(f32[1,1,2048]{2,1,0:T(1,128)} %get-tuple-element.484) | copy-start | bytes 24580
  455.4 212.4 %all-gather.45.cloned.1.call-start = ((), (), s32[]{:S(2)}) async-start(), calls=%async_computation.43 | async-start | bytes 2359296 | tf_op jit(solution)/shard_map/all_gather | solution.py:160
  533.2 26.0 collective-permute-start.3
  534.5 48.0 %collective-permute-start.4 = (bf16[256,2048]{1,0:T(8,128)(2,1)S(1)}, bf16[256,2048]{1,0:T(8,128)(2,1)}, u32[]{:S(2)}, u32[]{:S(2)}) collective-permute-start(bf16[256,2048]{1,0:T(8,128)(2,1)S(1)} %add_convert_fusion.2), channel_id=1, source_target_pairs={{0,3},{1,0},{2,1},{3,2},{4,7},{5,4},{6,5},{7,6},{8,11},{9,8},{10,9... | collective-permute-start | bytes 3145736 | tf_op jit(solution)/shard_map/ppermute | solution.py:184
  559.1 45.0 %collective-permute-start.5 = (bf16[256,2048]{1,0:T(8,128)(2,1)S(1)}, bf16[256,2048]{1,0:T(8,128)(2,1)}, u32[]{:S(2)}, u32[]{:S(2)}) collective-permute-start(bf16[256,2048]{1,0:T(8,128)(2,1)S(1)} %collective-permute-done.3), channel_id=1, source_target_pairs={{0,1},{1,2},{2,3},{3,0},{4,5},{5,6},{6,7},{7,4},{8,9},{9,10},{10,1... | collective-permute-start | bytes 3145736 | tf_op jit(solution)/shard_map/ppermute | solution.py:179
  559.2 192.0 %reduce-scatter.21.cloned.1.call-start = ((), (), s32[]{:S(2)}) async-start(), calls=%async_computation.19 | async-start | bytes 5242880 | tf_op jit(solution)/shard_map/reduce_scatter | solution.py:207
  674.2 77.0 %copy-start.9 = (f32[256,2048]{1,0:T(8,128)S(1)}, f32[256,2048]{1,0:T(8,128)}, u32[]{:S(2)}) copy-start(f32[256,2048]{1,0:T(8,128)} %copy-done.8) | copy-start | bytes 6291460
  674.2 147.6 %all-gather.47.cloned.1.call-start = ((), (), s32[]{:S(2)}) async-start(), calls=%async_computation.44 | async-start | bytes 12976128 | tf_op jit(solution)/shard_map/all_gather | solution.py:161
  676.9 77.1 %copy-start.65 = (f32[1,1,2048]{2,1,0:T(1,128)S(1)}, f32[1,1,2048]{2,1,0:T(1,128)}, u32[]{:S(2)}) copy-start(f32[1,1,2048]{2,1,0:T(1,128)} %get-tuple-element.477) | copy-start | bytes 24580
  676.9 77.1 %copy-start.74 = (f32[1,1,2048]{2,1,0:T(1,128)S(1)}, f32[1,1,2048]{2,1,0:T(1,128)}, u32[]{:S(2)}) copy-start(f32[1,1,2048]{2,1,0:T(1,128)} %get-tuple-element.481) | copy-start | bytes 24580
  676.9 227.4 %all-gather.25.cloned.1.call-start = ((), (), s32[]{:S(2)}) async-start(), calls=%async_computation.20 | async-start | bytes 5242880 | tf_op jit(solution)/shard_map/all_gather | solution.py:218
  755.4 229.8 %all-gather.27.cloned.1.call-start = ((), (), s32[]{:S(2)}) async-start(), calls=%async_computation.22 | async-start | bytes 5242880 | tf_op jit(solution)/shard_map/all_gather | solution.py:282
  756.2 274.3 %all-gather.49.cloned.1.call-start = ((), (), s32[]{:S(2)}) async-start(), calls=%async_computation.45 | async-start | bytes 6488064 | tf_op jit(solution)/shard_map/all_gather | solution.py:162
  756.8 383.2 %reduce-scatter.25.cloned.1.call-start = ((), (), s32[]{:S(2)}) async-start(), calls=%async_computation.23 | async-start | bytes 5242880 | tf_op jit(solution)/shard_map/reduce_scatter | solution.py:301
  1063.4 156.0 %reduce-scatter.23.cloned.1.call-start = ((), (), s32[]{:S(2)}) async-start(), calls=%async_computation.21 | async-start | bytes 5242880 | tf_op jit(solution)/shard_map/reduce_scatter | solution.py:229
  1081.3 138.1 %copy-start.24 = (bf16[256,2048]{1,0:T(8,128)(2,1)S(1)}, bf16[256,2048]{1,0:T(8,128)(2,1)}, u32[]{:S(2)}) copy-start(bf16[256,2048]{1,0:T(8,128)(2,1)} %param.27) | copy-start | bytes 3145732
  1081.4 224.1 %all-gather.29.cloned.1.call-start = ((), (), s32[]{:S(2)}) async-start(), calls=%async_computation.24 | async-start | bytes 5242880 | tf_op jit(solution)/shard_map/all_gather | solution.py:311
  1224.1 369.4 %reduce-scatter.27.cloned.1.call-start = ((), (), s32[]{:S(2)}) async-start(), calls=%async_computation.25 | async-start | bytes 5242880 | tf_op jit(solution)/shard_map/reduce_scatter | solution.py:334
  1224.2 89.6 %copy-start.54 = (f32[2,8,512,1]{2,1,3,0:T(8,128)S(1)}, f32[2,8,512,1]{2,1,3,0:T(8,128)}, u32[]{:S(2)}) copy-start(f32[2,8,512,1]{2,1,3,0:T(8,128)} %copy-done.53) | copy-start | bytes 98308
  1518.0 75.5 %copy-start.10 = (f32[256,2048]{1,0:T(8,128)S(1)}, f32[256,2048]{1,0:T(8,128)}, u32[]{:S(2)}) copy-start(f32[256,2048]{1,0:T(8,128)} %copy-done.8) | copy-start | bytes 6291460
  1518.0 75.5 %copy-start.64 = (f32[1,1,2048]{2,1,0:T(1,128)S(1)}, f32[1,1,2048]{2,1,0:T(1,128)}, u32[]{:S(2)}) copy-start(f32[1,1,2048]{2,1,0:T(1,128)} %get-tuple-element.480) | copy-start | bytes 24580
  1518.0 75.5 %copy-start.81 = (f32[256]{0:T(256)S(1)}, f32[256]{0:T(256)}, u32[]{:S(2)}) copy-start(f32[256]{0:T(256)} %copy-done.80) | copy-start | bytes 3076
  1518.0 75.5 %copy-start.87 = (f32[256]{0:T(256)S(1)}, f32[256]{0:T(256)}, u32[]{:S(2)}) copy-start(f32[256]{0:T(256)} %copy-done.86) | copy-start | bytes 3076
  1518.0 163.6 %all-gather.31.cloned.1.call-start = ((), (), s32[]{:S(2)}) async-start(), calls=%async_computation.26 | async-start | bytes 5242880 | tf_op jit(solution)/shard_map/all_gather | solution.py:282
  1600.2 189.9 %reduce-scatter.29.cloned.1.call-start = ((), (), s32[]{:S(2)}) async-start(), calls=%async_computation.27 | async-start | bytes 5242880 | tf_op jit(solution)/shard_map/reduce_scatter | solution.py:301
  1714.6 75.5 %copy-start.4 = (bf16[256,2048]{1,0:T(8,128)(2,1)S(1)}, bf16[256,2048]{1,0:T(8,128)(2,1)}, u32[]{:S(2)}) copy-start(bf16[256,2048]{1,0:T(8,128)(2,1)} %param.18) | copy-start | bytes 3145732
  1714.6 75.5 %copy-start.16 = (bf16[256,2048]{1,0:T(8,128)(2,1)S(1)}, bf16[256,2048]{1,0:T(8,128)(2,1)}, u32[]{:S(2)}) copy-start(bf16[256,2048]{1,0:T(8,128)(2,1)} %reduce-scatter.17.cloned.1.call-done) | copy-start | bytes 3145732
  1714.6 75.5 %copy-start.62 = (f32[1,1,2048]{2,1,0:T(1,128)S(1)}, f32[1,1,2048]{2,1,0:T(1,128)}, u32[]{:S(2)}) copy-start(f32[1,1,2048]{2,1,0:T(1,128)} %get-tuple-element.478) | copy-start | bytes 24580
  1714.7 75.5 %copy-start.79 = (f32[256]{0:T(256)S(1)}, f32[256]{0:T(256)}, u32[]{:S(2)}) copy-start(f32[256]{0:T(256)} %copy-done.78) | copy-start | bytes 3076
  1714.7 75.5 %copy-start.85 = (f32[256]{0:T(256)S(1)}, f32[256]{0:T(256)}, u32[]{:S(2)}) copy-start(f32[256]{0:T(256)} %copy-done.84) | copy-start | bytes 3076
  1714.7 182.9 %all-gather.33.cloned.1.call-start = ((), (), s32[]{:S(2)}) async-start(), calls=%async_computation.28 | async-start | bytes 5242880 | tf_op jit(solution)/shard_map/all_gather | solution.py:311
  1797.3 360.3 %reduce-scatter.47.cloned.1.call-start = ((), (), s32[]{:S(2)}) async-start(), calls=%async_computation.37 | async-start | bytes 6488064 | tf_op jit(solution)/shard_map/reduce_scatter | solution.py:356
  1808.1 349.5 %reduce-scatter.45.cloned.1.call-start = ((), (), s32[]{:S(2)}) async-start(), calls=%async_computation.36 | async-start | bytes 6488064 | tf_op jit(solution)/shard_map/reduce_scatter | solution.py:356
  1820.7 340.8 %reduce-scatter.43.cloned.1.call-start = ((), (), s32[]{:S(2)}) async-start(), calls=%async_computation.35 | async-start | bytes 12976128 | tf_op jit(solution)/shard_map/reduce_scatter | solution.py:353
  1855.3 328.5 %reduce-scatter.41.cloned.1.call-start = ((), (), s32[]{:S(2)}) async-start(), calls=%async_computation.34 | async-start | bytes 12976128 | tf_op jit(solution)/shard_map/reduce_scatter | solution.py:353
  1889.7 338.9 %reduce-scatter.39.cloned.1.call-start = ((), (), s32[]{:S(2)}) async-start(), calls=%async_computation.33 | async-start | bytes 2359296 | tf_op jit(solution)/shard_map/reduce_scatter | solution.py:350
  1897.6 375.4 %reduce-scatter.37.cloned.1.call-start = ((), (), s32[]{:S(2)}) async-start(), calls=%async_computation.32 | async-start | bytes 2359296 | tf_op jit(solution)/shard_map/reduce_scatter | solution.py:350
  1903.6 448.6 %reduce-scatter.31.cloned.1.call-start = ((), (), s32[]{:S(2)}) async-start(), calls=%async_computation.29 | async-start | bytes 5242880 | tf_op jit(solution)/shard_map/reduce_scatter | solution.py:334
  2130.7 287.1 %reduce-scatter.35.cloned.1.call-start = ((), (), s32[]{:S(2)}) async-start(), calls=%async_computation.31 | async-start | bytes 7077888 | tf_op jit(solution)/shard_map/reduce_scatter | solution.py:347
  2143.7 339.5 %reduce-scatter.33.cloned.1.call-start = ((), (), s32[]{:S(2)}) async-start(), calls=%async_computation.30 | async-start | bytes 7077888 | tf_op jit(solution)/shard_map/reduce_scatter | solution.py:347
  2156.7 456.3 %all-reduce.3.cloned.1.call-start = ((), (), s32[]{:S(2)}) async-start(), calls=%async_computation.46 | async-start | bytes 229376 | tf_op jit(solution)/shard_map/psum | solution.py:364
  2186.0 166.1 %copy-start.5 = (bf16[256,2048]{1,0:T(8,128)(2,1)S(1)}, bf16[256,2048]{1,0:T(8,128)(2,1)}, u32[]{:S(2)}) copy-start(bf16[256,2048]{1,0:T(8,128)(2,1)} %param.18) | copy-start | bytes 3145732
  2186.1 166.1 %copy-start.60 = (f32[1,1,2048]{2,1,0:T(1,128)S(1)}, f32[1,1,2048]{2,1,0:T(1,128)}, u32[]{:S(2)}) copy-start(f32[1,1,2048]{2,1,0:T(1,128)} %copy-done.59) | copy-start | bytes 24580
  2186.1 166.1 %copy-start.83 = (f32[256]{0:T(256)S(1)}, f32[256]{0:T(256)}, u32[]{:S(2)}) copy-start(f32[256]{0:T(256)} %copy-done.82) | copy-start | bytes 3076
  2186.1 166.1 %copy-start.89 = (f32[256]{0:T(256)S(1)}, f32[256]{0:T(256)}, u32[]{:S(2)}) copy-start(f32[256]{0:T(256)} %copy-done.88) | copy-start | bytes 3076
  2186.1 168.4 %copy-start.71 = (f32[2048]{0:T(1024)S(1)}, f32[2048]{0:T(1024)}, u32[]{:S(2)}) copy-start(f32[2048]{0:T(1024)} %get-tuple-element.313) | copy-start | bytes 24580
  2186.1 168.4 %copy-start.70 = (f32[2048]{0:T(1024)S(1)}, f32[2048]{0:T(1024)}, u32[]{:S(2)}) copy-start(f32[2048]{0:T(1024)} %get-tuple-element.326) | copy-start | bytes 24580
  2193.1 162.8 %copy-start.22 = (f32[256,2048]{1,0:T(8,128)S(1)}, f32[256,2048]{1,0:T(8,128)}, u32[]{:S(2)}) copy-start(f32[256,2048]{1,0:T(8,128)} %get-tuple-element.413) | copy-start | bytes 6291460
  (71 other events, 428.6 us)
Sparse Core Ops, SparseCore 0:
  11.1 49.1 all-gather.34
  62.7 28.1 all-gather.36
  164.5 78.3 reduce-scatter.16
  245.4 68.5 all-gather.38
  316.1 80.3 all-gather.22
  398.9 43.2 all-gather.40
  453.3 76.3 reduce-scatter.18
  532.1 47.5 all-gather.42
  581.6 28.9 all-gather.44
  674.3 76.7 reduce-scatter.20
  753.2 68.5 all-gather.46
  823.9 80.3 all-gather.24
  906.0 79.2 all-gather.26
  987.2 43.2 all-gather.48
  1063.5 76.3 reduce-scatter.24
  1142.1 77.2 reduce-scatter.22
  1224.2 81.2 all-gather.28
  1518.2 75.2 reduce-scatter.26
  1600.4 81.2 all-gather.30
  1714.8 75.2 reduce-scatter.28
  1797.4 81.2 all-gather.32
  1882.5 57.5 reduce-scatter.46
  1943.6 58.9 reduce-scatter.44
  2006.4 86.7 reduce-scatter.42
  2097.1 86.7 reduce-scatter.40
  2187.4 41.1 reduce-scatter.38
  2231.7 41.1 reduce-scatter.36
  2275.4 76.7 reduce-scatter.30
  2355.6 62.2 reduce-scatter.34
  2421.4 61.7 reduce-scatter.32
  2489.8 123.0 all-reduce.2
